TPU v7x, 512 devices: a whole 4x8x8 slice. The times are simulated.
512 devices in a mesh: row: 32 (over z_lo, x, core), col: 16 (over z_hi, y).
Axes of the slice: x: 4, y: 8, z: 8 (z_hi: 2, z_lo: 4; z = z_hi * 4 + z_lo), core: 2. Of those that a mesh axis runs over, the one named last changes fastest.
Arguments:
- state: float32 [32, 2, 16, 256, 256], P('row', None, 'col'), may hold values from -6 to 6
- a_tiles: float32 [32, 2, 16, 256, 256], P('row', None, 'col'), may hold values from -0.375 to 0.375
- inverses: float32 [32, 256, 256], P('row'), may hold values from -0.225 to 1.025
Outputs:
- state_out: float32 [32, 2, 16, 256, 256], P('row', None, 'col')
All inputs are finite; a program needn't handle non-finite values.
Results may differ from a plain program's by a relative error of at most 0.0001.
Values sent between devices are 32-bit elements; how exact they have to be, the bound alone decides.
A program may use at most 64 MiB of HBM per device.

v0:
```python
import jax
import jax.numpy as jnp
from jax import lax
from jax.sharding import PartitionSpec as P

FRONTS = 3
DOUBLINGS = 5
HIGH = lax.Precision.HIGHEST
shift_half = 0.5


def swapped(value, axis, stride):
    mask = 2**stride
    pairs = [(source, source ^ mask) for source in range(lax.axis_size(axis))]
    return lax.ppermute(value, axis, pairs)


def passed_along(block, axis, distance):
    devices = range(lax.axis_size(axis))
    route = [((i - distance) % len(devices), i) for i in devices]
    return lax.ppermute(block, axis, route)


def spread(value, axis, source):
    kept = jnp.where(lax.axis_index(axis) == source, value, 0).astype(value.dtype)
    return lax.psum(kept, axis)


def product(left, right):
    return jnp.dot(left, right, precision=HIGH, preferred_element_type=jnp.float32)


def product_transposed(left, right):
    return lax.dot_general(
        left, right, (((1,), (1,)), ((), ())), precision=HIGH, preferred_element_type=jnp.float32
    )


def batched_product(left, right):
    return jnp.einsum(
        "nab,nbc->nac", left, right, precision=HIGH, preferred_element_type=jnp.float32
    )


def across_cols(pieces):
    return lax.all_to_all(pieces, "col", split_axis=1, concat_axis=1, tiled=True)


def mirrored(tile_set):
    slot_count = tile_set.shape[0]
    tile_order = tile_set.shape[1]
    col_count = lax.axis_size("col")
    slab_rows = tile_order // col_count
    section_one = across_cols(tile_set.reshape(slot_count, col_count, slab_rows, tile_order))
    by_target = section_one.reshape(slot_count * col_count, slab_rows, tile_order)
    section_two = lax.all_to_all(by_target, "row", split_axis=0, concat_axis=0, tiled=True)
    section_three = across_cols(section_two.reshape(slot_count, col_count, slab_rows, tile_order))
    return section_three.reshape(slot_count, tile_order, tile_order)


def flipped(tile_set, col_count):
    levels = col_count.bit_length() - 1
    for bit_pos in range(levels):
        tile_set = swapped(tile_set, "col", bit_pos)
    return tile_set


def per_device(state, a_tiles, inverses):
    slot_count = state.shape[1]
    tile_order = state.shape[3]
    col_count = lax.axis_size("col")
    height = lax.axis_size("row")
    row_here = lax.axis_index("row")
    col_here = lax.axis_index("col")
    current = state.reshape(slot_count, tile_order, tile_order)
    coupling = a_tiles.reshape(slot_count, tile_order, tile_order)
    own_inverse = inverses.reshape(tile_order, tile_order)
    identity_tile = jnp.eye(tile_order, dtype=jnp.float32)
    left_powers = [identity_tile - shift_half * own_inverse]
    for level in range(DOUBLINGS - 1):
        left_powers.append(product(left_powers[-1], left_powers[-1]))
    column_inverse = mirrored(jnp.broadcast_to(own_inverse, (slot_count, tile_order, tile_order)))
    right_list = [identity_tile[None] - shift_half * column_inverse]
    for level in range(DOUBLINGS - 1):
        right_list.append(batched_product(right_list[-1], right_list[-1]))
    right_powers = jnp.stack(right_list)
    tile_cols = jnp.arange(slot_count, dtype=jnp.int32) * col_count + col_here
    tile_sum = row_here + tile_cols
    for front_step in range(FRONTS):
        front_sum = height - 1 - front_step
        source_a = flipped(coupling, col_count)
        if front_step > 0:
            source_a = passed_along(source_a, "col", -front_step)
        front_col = front_sum - row_here
        front_slot = jnp.clip(front_col // col_count, 0, slot_count - 1)
        own_tile = lax.dynamic_index_in_dim(current, front_slot, 0, keepdims=False)
        mirror = mirrored(current)
        far_tile = lax.dynamic_index_in_dim(mirror, front_slot, 0, keepdims=False)
        right_side = own_tile + far_tile.T
        right_inverse = lax.dynamic_index_in_dim(column_inverse, front_slot, 0, keepdims=False)
        powers_here = lax.dynamic_index_in_dim(right_powers, front_slot, 1, keepdims=False)
        solution = shift_half * product_transposed(product(own_inverse, right_side), right_inverse)
        for level in range(DOUBLINGS):
            solution = solution + product_transposed(
                product(left_powers[level], solution), powers_here[level]
            )
        passed = []
        for slot_pos in range(slot_count):
            root_row = jnp.clip(front_sum - tile_cols[slot_pos], 0, height - 1)
            passed.append(spread(solution, "row", root_row))
        below_rows = front_sum - tile_cols
        a_slot = jnp.clip(below_rows // col_count, 0, slot_count - 1)
        a_pick = jnp.take(source_a, a_slot, axis=0)
        update = batched_product(a_pick, jnp.stack(passed))
        shrink = (tile_sum < front_sum)[:, None, None]
        place = (tile_sum == front_sum)[:, None, None]
        current = jnp.where(shrink, current - update, jnp.where(place, solution[None], current))
    return current.reshape(state.shape)


def solution(mesh):
    in_specs = (
        P("row", None, "col", None, None),
        P("row", None, "col", None, None),
        P("row", None, None),
    )
    out_specs = P("row", None, "col", None, None)
    return jax.shard_map(
        per_device, mesh=mesh, in_specs=in_specs, out_specs=out_specs, check_vma=False
    )
```

profile of v0, /device:TPU:1, one launch (start us, length us, event | category | flops | bytes accessed | tf_op | source)
XLA Modules:
  0.0 1221.0 jit_solution(3985047102242037960)
XLA Ops:
  7.6 34.1 %all_to_all.60 = f32[2,16,16,256]{3,2,0,1:T(8,128)S(1)} all-to-all(f32[2,16,16,256]{3,2,0,1:T(8,128)S(1)} %copy.25), channel_id=1, replica_groups=mesh['row'=32,'col'=16] {'col'}, dimensions={1} | all-to-all | bytes 1048576 | tf_op jit(solution)/shard_map/all_to_all | solution.py:46
  50.0 16.1 %all-to-all-done.3 = f32[2,16,16,256]{3,2,0,1:T(8,128)S(1)} async-done(((f32[2,16,16,256]{3,2,0,1:T(8,128)}), f32[2,16,16,256]{3,2,0,1:T(8,128)S(1)}, u32[]{:S(2)}, u32[]{:S(2)}) %all-to-all-start.3) | async-done | bytes 524320 | tf_op jit(solution)/shard_map/all_to_all | solution.py:46
  66.1 10.6 all-to-all-start.1
  77.6 15.6 %all-to-all-done.1 = f32[32,16,256]{2,1,0:T(8,128)S(1)} async-done(((f32[32,16,256]{2,1,0:T(8,128)}), f32[32,16,256]{2,1,0:T(8,128)S(1)}, u32[]{:S(2)}, u32[]{:S(2)}) %all-to-all-start.1) | async-done | bytes 524320 | tf_op jit(solution)/shard_map/all_to_all | solution.py:56
  101.4 12.4 %all-to-all-done.4 = f32[32,16,256]{2,1,0:T(8,128)S(1)} async-done(((f32[32,16,256]{2,1,0:T(8,128)}), f32[32,16,256]{2,1,0:T(8,128)S(1)}, u32[]{:S(2)}, u32[]{:S(2)}) %all-to-all-start.4) | async-done | bytes 524320 | tf_op jit(solution)/shard_map/all_to_all | solution.py:56
  124.1 13.2 %all-to-all-done.2 = f32[2,16,16,256]{3,2,0,1:T(8,128)S(1)} async-done(((f32[2,16,16,256]{3,2,0,1:T(8,128)}), f32[2,16,16,256]{3,2,0,1:T(8,128)S(1)}, u32[]{:S(2)}, u32[]{:S(2)}) %all-to-all-start.2) | async-done | bytes 524320 | tf_op jit(solution)/shard_map/all_to_all | solution.py:46
  137.4 5.7 all-to-all-start.5
  143.8 15.3 %collective-permute-done.1 = f32[2,256,256]{2,1,0:T(8,128)} collective-permute-done((f32[2,256,256]{2,1,0:T(8,128)}, f32[2,256,256]{2,1,0:T(8,128)}, u32[]{:S(2)}, u32[]{:S(2)}) %collective-permute-start.1) | collective-permute-done | bytes 524320 | tf_op jit(solution)/shard_map/ppermute | solution.py:15
  159.0 8.0 collective-permute-start.2
  169.1 20.2 %collective-permute-done.2 = f32[2,256,256]{2,1,0:T(8,128)} collective-permute-done((f32[2,256,256]{2,1,0:T(8,128)}, f32[2,256,256]{2,1,0:T(8,128)}, u32[]{:S(2)}, u32[]{:S(2)}) %collective-permute-start.2) | collective-permute-done | bytes 524320 | tf_op jit(solution)/shard_map/ppermute | solution.py:15
  200.8 11.9 collective-permute-done.3
  215.1 269.7 %all-reduce.11.cloned.1.call-done = (f32[1,256,256]{2,1,0:T(8,128)}, f32[1,256,256]{2,1,0:T(8,128)}) async-done(((f32[1,256,256]{2,1,0:T(8,128)}, f32[1,256,256]{2,1,0:T(8,128)}), (f32[1,256,256]{2,1,0:T(8,128)}, f32[1,256,256]{2,1,0:T(8,128)})) %all-reduce.11.cloned.1.call-update) | async-done | bytes 524304 | tf_op jit(solution)/shard_map/psum | solution.py:26
  486.7 26.0 %all_to_all.61 = f32[2,16,16,256]{3,2,0,1:T(8,128)S(1)} all-to-all(f32[2,16,16,256]{3,2,0,1:T(8,128)S(1)} %copy.34), channel_id=1, replica_groups=mesh['row'=32,'col'=16] {'col'}, dimensions={1} | all-to-all | bytes 1048576 | tf_op jit(solution)/shard_map/all_to_all | solution.py:46
  512.8 23.9 %all_to_all.62 = f32[32,16,256]{2,1,0:T(8,128)S(1)} all-to-all(f32[32,16,256]{2,1,0:T(8,128)S(1)} %bitcast.223), channel_id=1, replica_groups=mesh['row'=32,'col'=16] {'row'}, dimensions={0} | all-to-all | bytes 1048576 | tf_op jit(solution)/shard_map/all_to_all | solution.py:56
  543.8 9.5 collective-permute-start.4
  553.3 8.2 all-to-all-done.8
  568.1 9.1 collective-permute-done.4
  579.5 270.4 %all-reduce.9.cloned.1.call-done = (f32[1,256,256]{2,1,0:T(8,128)}, f32[1,256,256]{2,1,0:T(8,128)}) async-done(((f32[1,256,256]{2,1,0:T(8,128)}, f32[1,256,256]{2,1,0:T(8,128)}), (f32[1,256,256]{2,1,0:T(8,128)}, f32[1,256,256]{2,1,0:T(8,128)})) %all-reduce.9.cloned.1.call-update) | async-done | bytes 524304 | tf_op jit(solution)/shard_map/psum | solution.py:26
  851.9 26.0 %all_to_all.63 = f32[2,16,16,256]{3,2,0,1:T(8,128)S(1)} all-to-all(f32[2,16,16,256]{3,2,0,1:T(8,128)S(1)} %copy.39), channel_id=1, replica_groups=mesh['row'=32,'col'=16] {'col'}, dimensions={1} | all-to-all | bytes 1048576 | tf_op jit(solution)/shard_map/all_to_all | solution.py:46
  878.0 23.9 %all_to_all.64 = f32[32,16,256]{2,1,0:T(8,128)S(1)} all-to-all(f32[32,16,256]{2,1,0:T(8,128)S(1)} %bitcast.225), channel_id=1, replica_groups=mesh['row'=32,'col'=16] {'row'}, dimensions={0} | all-to-all | bytes 1048576 | tf_op jit(solution)/shard_map/all_to_all | solution.py:56
  909.0 10.5 collective-permute-start.5
  919.4 7.3 all-to-all-done.11
  933.3 11.4 collective-permute-done.5
  945.3 266.6 %all-reduce.7.cloned.1.call-done = (f32[1,256,256]{2,1,0:T(8,128)}, f32[1,256,256]{2,1,0:T(8,128)}) async-done(((f32[1,256,256]{2,1,0:T(8,128)}, f32[1,256,256]{2,1,0:T(8,128)}), (f32[1,256,256]{2,1,0:T(8,128)}, f32[1,256,256]{2,1,0:T(8,128)})) %all-reduce.7.cloned.1.call-update) | async-done | bytes 524304 | tf_op jit(solution)/shard_map/psum | solution.py:26
  (120 shorter events, 77.5 us)
Async XLA Ops:
  43.5 53.8 %copy-start.5 = (f32[1,2,1,256,256]{4,3,2,1,0:T(8,128)S(1)}, f32[1,2,1,256,256]{4,3,2,1,0:T(8,128)}, u32[]{:S(2)}) copy-start(f32[1,2,1,256,256]{4,3,2,1,0:T(8,128)} %param.6) | copy-start | bytes 1572868
  43.5 22.6 %all-to-all-start.3 = ((f32[2,16,16,256]{3,2,0,1:T(8,128)}), f32[2,16,16,256]{3,2,0,1:T(8,128)S(1)}, u32[]{:S(2)}, u32[]{:S(2)}) async-start(f32[2,16,16,256]{3,2,0,1:T(8,128)} %broadcast_in_dim.91), calls=%async_computation.3 | async-start | bytes 1048576 | tf_op jit(solution)/shard_map/all_to_all | solution.py:46
  66.1 52.2 %copy-start = (f32[1,256,256]{2,1,0:T(8,128)S(1)}, f32[1,256,256]{2,1,0:T(8,128)}, u32[]{:S(2)}) copy-start(f32[1,256,256]{2,1,0:T(8,128)} %param.7) | copy-start | bytes 786436
  66.1 27.1 %all-to-all-start.1 = ((f32[32,16,256]{2,1,0:T(8,128)}), f32[32,16,256]{2,1,0:T(8,128)S(1)}, u32[]{:S(2)}, u32[]{:S(2)}) async-start(f32[32,16,256]{2,1,0:T(8,128)} %bitcast.5), calls=%async_computation.1 | async-start | bytes 1048576 | tf_op jit(solution)/shard_map/all_to_all | solution.py:56
  93.2 20.6 %all-to-all-start.4 = ((f32[32,16,256]{2,1,0:T(8,128)}), f32[32,16,256]{2,1,0:T(8,128)S(1)}, u32[]{:S(2)}, u32[]{:S(2)}) async-start(f32[32,16,256]{2,1,0:T(8,128)} %bitcast.12), calls=%async_computation.4 | async-start | bytes 1048576 | tf_op jit(solution)/shard_map/all_to_all | solution.py:56
  97.3 21.4 %collective-permute-start = (f32[2,256,256]{2,1,0:T(8,128)S(1)}, f32[2,256,256]{2,1,0:T(8,128)}, u32[]{:S(2)}, u32[]{:S(2)}) collective-permute-start(f32[2,256,256]{2,1,0:T(8,128)S(1)} %bitcast.230), channel_id=1, source_target_pairs={{0,1},{1,0},{2,3},{3,2},{4,5},{5,4},{6,7},{7,6},{8,9},{9,8},{10,11... | collective-permute-start | bytes 1572872 | tf_op jit(solution)/shard_map/ppermute | solution.py:15
  113.7 23.6 %all-to-all-start.2 = ((f32[2,16,16,256]{3,2,0,1:T(8,128)}), f32[2,16,16,256]{3,2,0,1:T(8,128)S(1)}, u32[]{:S(2)}, u32[]{:S(2)}) async-start(f32[2,16,16,256]{3,2,0,1:T(8,128)} %copy.27), calls=%async_computation.2 | async-start | bytes 1048576 | tf_op jit(solution)/shard_map/all_to_all | solution.py:46
  118.7 40.3 %collective-permute-start.1 = (f32[2,256,256]{2,1,0:T(8,128)}, f32[2,256,256]{2,1,0:T(8,128)}, u32[]{:S(2)}, u32[]{:S(2)}) collective-permute-start(f32[2,256,256]{2,1,0:T(8,128)} %collective-permute-done), channel_id=1, source_target_pairs={{0,2},{1,3},{2,0},{3,1},{4,6},{5,7},{6,4},{7,5},{8,10},{9,11},{10,... | collective-permute-start | bytes 1572872 | tf_op jit(solution)/shard_map/ppermute | solution.py:15
  124.1 67.4 %copy-start.4 = (f32[1,2,1,256,256]{4,3,2,1,0:T(8,128)S(1)}, f32[1,2,1,256,256]{4,3,2,1,0:T(8,128)}, u32[]{:S(2)}) copy-start(f32[1,2,1,256,256]{4,3,2,1,0:T(8,128)} %param.5) | copy-start | bytes 1572868
  137.4 54.8 %all-to-all-start.5 = ((f32[2,16,16,256]{3,2,0,1:T(8,128)}), f32[2,16,16,256]{3,2,0,1:T(8,128)S(1)}, u32[]{:S(2)}, u32[]{:S(2)}) async-start(f32[2,16,16,256]{3,2,0,1:T(8,128)} %copy.31), calls=%async_computation.5 | async-start | bytes 1048576 | tf_op jit(solution)/shard_map/all_to_all | solution.py:46
  143.1 341.7 %all-reduce.11.cloned.1.call-start = ((), (), s32[]{:S(2)}) async-start(), calls=%async_computation.14 | async-start | bytes 1048576 | tf_op jit(solution)/shard_map/psum | solution.py:26
  159.0 30.2 %collective-permute-start.2 = (f32[2,256,256]{2,1,0:T(8,128)}, f32[2,256,256]{2,1,0:T(8,128)}, u32[]{:S(2)}, u32[]{:S(2)}) collective-permute-start(f32[2,256,256]{2,1,0:T(8,128)} %collective-permute-done.1), channel_id=1, source_target_pairs={{0,4},{1,5},{2,6},{3,7},{4,0},{5,1},{6,2},{7,3},{8,12},{9,13},{10,... | collective-permute-start | bytes 1572872 | tf_op jit(solution)/shard_map/ppermute | solution.py:15
  189.3 23.4 %collective-permute-start.3 = (f32[2,256,256]{2,1,0:T(8,128)}, f32[2,256,256]{2,1,0:T(8,128)}, u32[]{:S(2)}, u32[]{:S(2)}) collective-permute-start(f32[2,256,256]{2,1,0:T(8,128)} %collective-permute-done.2), channel_id=1, source_target_pairs={{0,8},{1,9},{2,10},{3,11},{4,12},{5,13},{6,14},{7,15},{8,0},{9,1},... | collective-permute-start | bytes 1572872 | tf_op jit(solution)/shard_map/ppermute | solution.py:15
  196.1 3.3 copy-start.1
  537.5 24.0 %all-to-all-start.8 = ((f32[2,16,16,256]{3,2,0,1:T(8,128)}), f32[2,16,16,256]{3,2,0,1:T(8,128)S(1)}, u32[]{:S(2)}, u32[]{:S(2)}) async-start(f32[2,16,16,256]{3,2,0,1:T(8,128)} %copy.36), calls=%async_computation.8 | async-start | bytes 1048576 | tf_op jit(solution)/shard_map/all_to_all | solution.py:46
  542.4 307.6 %all-reduce.9.cloned.1.call-start = ((), (), s32[]{:S(2)}) async-start(), calls=%async_computation.13 | async-start | bytes 1048576 | tf_op jit(solution)/shard_map/psum | solution.py:26
  543.8 33.4 %collective-permute-start.4 = (f32[2,256,256]{2,1,0:T(8,128)}, f32[2,256,256]{2,1,0:T(8,128)}, u32[]{:S(2)}, u32[]{:S(2)}) collective-permute-start(f32[2,256,256]{2,1,0:T(8,128)} %collective-permute-done.3), channel_id=1, source_target_pairs={{1,0},{2,1},{3,2},{4,3},{5,4},{6,5},{7,6},{8,7},{9,8},{10,9},{11,1... | collective-permute-start | bytes 1572872 | tf_op jit(solution)/shard_map/ppermute | solution.py:21
  561.7 1.7 copy-start.2
  902.8 24.0 %all-to-all-start.11 = ((f32[2,16,16,256]{3,2,0,1:T(8,128)}), f32[2,16,16,256]{3,2,0,1:T(8,128)S(1)}, u32[]{:S(2)}, u32[]{:S(2)}) async-start(f32[2,16,16,256]{3,2,0,1:T(8,128)} %copy.41), calls=%async_computation.11 | async-start | bytes 1048576 | tf_op jit(solution)/shard_map/all_to_all | solution.py:46
  907.6 304.3 %all-reduce.7.cloned.1.call-start = ((), (), s32[]{:S(2)}) async-start(), calls=%async_computation.12 | async-start | bytes 1048576 | tf_op jit(solution)/shard_map/psum | solution.py:26
  909.0 35.8 %collective-permute-start.5 = (f32[2,256,256]{2,1,0:T(8,128)}, f32[2,256,256]{2,1,0:T(8,128)S(1)}, u32[]{:S(2)}, u32[]{:S(2)}) collective-permute-start(f32[2,256,256]{2,1,0:T(8,128)} %collective-permute-done.3), channel_id=1, source_target_pairs={{2,0},{3,1},{4,2},{5,3},{6,4},{7,5},{8,6},{9,7},{10,8},{11,9},{12,... | collective-permute-start | bytes 1572872 | tf_op jit(solution)/shard_map/ppermute | solution.py:21
  926.9 1.7 copy-start.3
Sparse Core Ops, SparseCore 0:
  200.8 283.9 all-reduce.10
  568.1 281.8 all-reduce.8
  933.3 278.5 all-reduce.6
where the time goes:
time: 1220 us
  waiting for transfers between devices  948 us (78%)
  blocking collectives  134 us (11%)
  starting transfers between devices  77.8 us (6%)
  matrix products  26.2 us (2%)
  between operations  17.7 us (1%)
  local copies, waits for them, and re-layouts  14.9 us (1%)
    psum x3, waiting for transfers between devices, spread(): return lax.psum(kept, axis)  807 us
    all_to_all x3, blocking collectives, across_cols(): lax.all_to_all(pieces, 'col', split_axis=1, concat_axis=1, tiled=True)  86.2 us
    all_to_all x2, blocking collectives, mirrored(): lax.all_to_all(by_target, 'row', split_axis=0, concat_axis=0, tiled=True)  47.8 us
    ppermute x4, waiting for transfers between devices, swapped(): return lax.ppermute(value, axis, pairs)  47.4 us
    all_to_all x5, waiting for transfers between devices, across_cols(): lax.all_to_all(pieces, 'col', split_axis=1, concat_axis=1, tiled=True)  44.9 us
    all_to_all x2, waiting for transfers between devices, mirrored(): lax.all_to_all(by_target, 'row', split_axis=0, concat_axis=0, tiled=True)  28 us
    all_to_all x5, starting transfers between devices, across_cols(): lax.all_to_all(pieces, 'col', split_axis=1, concat_axis=1, tiled=True)  25.6 us
  transfers between devices with their start and end apart: 16, of which 14 were waited for; matrix products, arithmetic and copies ran while one was open for 3% of the time, Pallas kernels for 0%

commit v1 on v0

--- a/solution.py
+++ b/solution.py
@@ -23,7 +23,7 @@
 
 def spread(value, axis, source):
     kept = jnp.where(lax.axis_index(axis) == source, value, 0).astype(value.dtype)
-    return lax.psum(kept, axis)
+    return jnp.sum(lax.all_gather(kept, axis), axis=0)
 
 
 def product(left, right):

time: 1220 us -> 834 us (0.68)
  waiting for transfers between devices: 948 us -> 540 us
  other arithmetic: 2.77 us -> 26.6 us
    psum x3 -> x0, waiting for transfers between devices: 807 us -> none  [spread(): return lax.psum(kept, axis)]
    all_gather x0 -> x6, waiting for transfers between devices: none -> 309 us  [spread(): return jnp.sum(lax.all_gather(kept, axis), axis=0)]
    all_to_all x5, waiting for transfers between devices: 44.9 us -> 81.3 us  [across_cols(): lax.all_to_all(pieces, 'col', split_axis=1, concat_axis=1, tiled=True)]
    ppermute x4, waiting for transfers between devices: 47.4 us -> 79.2 us  [swapped(): return lax.ppermute(value, axis, pairs)]
    reduce_sum x0 -> x6, other arithmetic: none -> 26.4 us  [spread(): return jnp.sum(lax.all_gather(kept, axis), axis=0)]
    ppermute x2, waiting for transfers between devices: 20.5 us -> 37.9 us  [passed_along(): return lax.ppermute(block, axis, route)]
  transfers between devices with their start and end apart: 16 -> 19, of which waited for: 14 -> 18; matrix products, arithmetic and copies ran while one was open for 3% -> 3% of each run, Pallas kernels for 0% -> 0%
where the time goes in v1:
time: 834 us; the launch traced here: 832 us
  waiting for transfers between devices  540 us (65%)
  blocking collectives  137 us (16%)
  starting transfers between devices  68.3 us (8%)
  matrix products  29.2 us (4%)
  other arithmetic  26.6 us (3%)
  between operations  18.3 us (2%)
  local copies, waits for them, and re-layouts  12.4 us (1%)
    all_gather x6, waiting for transfers between devices, spread(): return jnp.sum(lax.all_gather(kept, axis), axis=0)  309 us
    all_to_all x3, blocking collectives, across_cols(): lax.all_to_all(pieces, 'col', split_axis=1, concat_axis=1, tiled=True)  89.2 us
    all_to_all x5, waiting for transfers between devices, across_cols(): lax.all_to_all(pieces, 'col', split_axis=1, concat_axis=1, tiled=True)  81.3 us
    ppermute x4, waiting for transfers between devices, swapped(): return lax.ppermute(value, axis, pairs)  79.2 us
    all_to_all x2, blocking collectives, mirrored(): lax.all_to_all(by_target, 'row', split_axis=0, concat_axis=0, tiled=True)  48.1 us
    ppermute x2, waiting for transfers between devices, passed_along(): return lax.ppermute(block, axis, route)  37.9 us
    all_to_all x2, waiting for transfers between devices, mirrored(): lax.all_to_all(by_target, 'row', split_axis=0, concat_axis=0, tiled=True)  31.1 us
    reduce_sum x6, other arithmetic, spread(): return jnp.sum(lax.all_gather(kept, axis), axis=0)  26.4 us
  transfers between devices with their start and end apart: 19, of which 18 were waited for; matrix products, arithmetic and copies ran while one was open for 3% of the time, Pallas kernels for 0%

profile of v1, /device:TPU:1, one launch (start us, length us, event | category | flops | bytes accessed | tf_op | source)
XLA Modules:
  0.0 832.2 jit_solution(12870317490297075241)
XLA Ops:
  7.6 34.1 %all_to_all.60 = f32[2,16,16,256]{3,2,0,1:T(8,128)S(1)} all-to-all(f32[2,16,16,256]{3,2,0,1:T(8,128)S(1)} %copy.25), channel_id=1, replica_groups=mesh['row'=32,'col'=16] {'col'}, dimensions={1} | all-to-all | bytes 1048576 | tf_op jit(solution)/shard_map/all_to_all | solution.py:46
  49.9 16.1 %all-to-all-done.3 = f32[2,16,16,256]{3,2,0,1:T(8,128)S(1)} async-done(((f32[2,16,16,256]{3,2,0,1:T(8,128)}), f32[2,16,16,256]{3,2,0,1:T(8,128)S(1)}, u32[]{:S(2)}, u32[]{:S(2)}) %all-to-all-start.3) | async-done | bytes 524320 | tf_op jit(solution)/shard_map/all_to_all | solution.py:46
  66.0 10.6 %all-to-all-start.1 = ((f32[32,16,256]{2,1,0:T(8,128)}), f32[32,16,256]{2,1,0:T(8,128)S(1)}, u32[]{:S(2)}, u32[]{:S(2)}) async-start(f32[32,16,256]{2,1,0:T(8,128)} %bitcast.5), calls=%async_computation.1 | async-start | bytes 1048576 | tf_op jit(solution)/shard_map/all_to_all | solution.py:56
  77.5 15.6 %all-to-all-done.1 = f32[32,16,256]{2,1,0:T(8,128)S(1)} async-done(((f32[32,16,256]{2,1,0:T(8,128)}), f32[32,16,256]{2,1,0:T(8,128)S(1)}, u32[]{:S(2)}, u32[]{:S(2)}) %all-to-all-start.1) | async-done | bytes 524320 | tf_op jit(solution)/shard_map/all_to_all | solution.py:56
  98.1 15.6 %all-to-all-done.4 = f32[32,16,256]{2,1,0:T(8,128)S(1)} async-done(((f32[32,16,256]{2,1,0:T(8,128)}), f32[32,16,256]{2,1,0:T(8,128)S(1)}, u32[]{:S(2)}, u32[]{:S(2)}) %all-to-all-start.4) | async-done | bytes 524320 | tf_op jit(solution)/shard_map/all_to_all | solution.py:56
  119.8 17.4 %all-to-all-done.2 = f32[2,16,16,256]{3,2,0,1:T(8,128)S(1)} async-done(((f32[2,16,16,256]{3,2,0,1:T(8,128)}), f32[2,16,16,256]{3,2,0,1:T(8,128)S(1)}, u32[]{:S(2)}, u32[]{:S(2)}) %all-to-all-start.2) | async-done | bytes 524320 | tf_op jit(solution)/shard_map/all_to_all | solution.py:46
  147.1 12.7 %all-to-all-done.5 = f32[2,16,16,256]{3,2,0,1:T(8,128)S(1)} async-done(((f32[2,16,16,256]{3,2,0,1:T(8,128)}), f32[2,16,16,256]{3,2,0,1:T(8,128)S(1)}, u32[]{:S(2)}, u32[]{:S(2)}) %all-to-all-start.5) | async-done | bytes 524320 | tf_op jit(solution)/shard_map/all_to_all | solution.py:46
  186.0 22.6 %collective-permute-done.1 = f32[2,256,256]{2,1,0:T(8,128)S(1)} collective-permute-done((f32[2,256,256]{2,1,0:T(8,128)S(1)}, f32[2,256,256]{2,1,0:T(8,128)S(1)}, u32[]{:S(2)}, u32[]{:S(2)}) %collective-permute-start.1) | collective-permute-done | bytes 524320 | tf_op jit(solution)/shard_map/ppermute | solution.py:15
  208.7 9.2 %collective-permute-start.2 = (f32[2,256,256]{2,1,0:T(8,128)S(1)}, f32[2,256,256]{2,1,0:T(8,128)S(1)}, u32[]{:S(2)}, u32[]{:S(2)}) collective-permute-start(f32[2,256,256]{2,1,0:T(8,128)S(1)} %collective-permute-done.1), channel_id=1, source_target_pairs={{0,4},{1,5},{2,6},{3,7},{4,0},{5,1},{6,2},{7,3},{8,12},{9,13},{10,... | collective-permute-start | bytes 1572872 | tf_op jit(solution)/shard_map/ppermute | solution.py:15
  217.9 23.1 %collective-permute-done.2 = f32[2,256,256]{2,1,0:T(8,128)S(1)} collective-permute-done((f32[2,256,256]{2,1,0:T(8,128)S(1)}, f32[2,256,256]{2,1,0:T(8,128)S(1)}, u32[]{:S(2)}, u32[]{:S(2)}) %collective-permute-start.2) | collective-permute-done | bytes 524320 | tf_op jit(solution)/shard_map/ppermute | solution.py:15
  244.0 24.4 %collective-permute-done.3 = f32[2,256,256]{2,1,0:T(8,128)S(1)} collective-permute-done((f32[2,256,256]{2,1,0:T(8,128)S(1)}, f32[2,256,256]{2,1,0:T(8,128)S(1)}, u32[]{:S(2)}, u32[]{:S(2)}) %collective-permute-start.3) | collective-permute-done | bytes 524320 | tf_op jit(solution)/shard_map/ppermute | solution.py:15
  273.7 57.1 %all-gather.15.cloned.1.call-done = f32[8192,256]{1,0:T(8,128)} async-done(((f32[256,256]{1,0:T(8,128)}), f32[8192,256]{1,0:T(8,128)}) %all-gather.15.cloned.1.call-update) | async-done | bytes 8388624 | tf_op jit(solution)/shard_map/all_gather | solution.py:26
  337.3 27.6 %all_to_all.61 = f32[2,16,16,256]{3,2,0,1:T(8,128)S(1)} all-to-all(f32[2,16,16,256]{3,2,0,1:T(8,128)S(1)} %copy.34), channel_id=1, replica_groups=mesh['row'=32,'col'=16] {'col'}, dimensions={1} | all-to-all | bytes 1048576 | tf_op jit(solution)/shard_map/all_to_all | solution.py:46
  364.9 24.1 %all_to_all.62 = f32[32,16,256]{2,1,0:T(8,128)S(1)} all-to-all(f32[32,16,256]{2,1,0:T(8,128)S(1)} %bitcast.235), channel_id=1, replica_groups=mesh['row'=32,'col'=16] {'row'}, dimensions={0} | all-to-all | bytes 1048576 | tf_op jit(solution)/shard_map/all_to_all | solution.py:56
  395.7 17.7 %all-to-all-done.8 = f32[2,16,16,256]{3,2,0,1:T(8,128)S(1)} async-done(((f32[2,16,16,256]{3,2,0,1:T(8,128)}), f32[2,16,16,256]{3,2,0,1:T(8,128)S(1)}, u32[]{:S(2)}, u32[]{:S(2)}) %all-to-all-start.8) | async-done | bytes 524320 | tf_op jit(solution)/shard_map/all_to_all | solution.py:46
  424.7 16.2 %collective-permute-done.4 = f32[2,256,256]{2,1,0:T(8,128)} collective-permute-done((f32[2,256,256]{2,1,0:T(8,128)S(1)}, f32[2,256,256]{2,1,0:T(8,128)}, u32[]{:S(2)}, u32[]{:S(2)}) %collective-permute-start.4) | collective-permute-done | bytes 524320 | tf_op jit(solution)/shard_map/ppermute | solution.py:21
  442.5 43.1 %all-gather.17.cloned.1.call-done = f32[8192,256]{1,0:T(8,128)} async-done(((f32[256,256]{1,0:T(8,128)}), f32[8192,256]{1,0:T(8,128)}) %all-gather.17.cloned.1.call-update) | async-done | bytes 8388624 | tf_op jit(solution)/shard_map/all_gather | solution.py:26
  490.3 84.1 %all-gather.19.cloned.1.call-done = f32[8192,256]{1,0:T(8,128)} async-done(((f32[256,256]{1,0:T(8,128)}), f32[8192,256]{1,0:T(8,128)}) %all-gather.19.cloned.1.call-update) | async-done | bytes 8388624 | tf_op jit(solution)/shard_map/all_gather | solution.py:26
  580.9 27.6 %all_to_all.63 = f32[2,16,16,256]{3,2,0,1:T(8,128)S(1)} all-to-all(f32[2,16,16,256]{3,2,0,1:T(8,128)S(1)} %copy.39), channel_id=1, replica_groups=mesh['row'=32,'col'=16] {'col'}, dimensions={1} | all-to-all | bytes 1048576 | tf_op jit(solution)/shard_map/all_to_all | solution.py:46
  608.5 24.1 %all_to_all.64 = f32[32,16,256]{2,1,0:T(8,128)S(1)} all-to-all(f32[32,16,256]{2,1,0:T(8,128)S(1)} %bitcast.237), channel_id=1, replica_groups=mesh['row'=32,'col'=16] {'row'}, dimensions={0} | all-to-all | bytes 1048576 | tf_op jit(solution)/shard_map/all_to_all | solution.py:56
  639.6 17.4 %all-to-all-done.11 = f32[2,16,16,256]{3,2,0,1:T(8,128)S(1)} async-done(((f32[2,16,16,256]{3,2,0,1:T(8,128)}), f32[2,16,16,256]{3,2,0,1:T(8,128)S(1)}, u32[]{:S(2)}, u32[]{:S(2)}) %all-to-all-start.11) | async-done | bytes 524320 | tf_op jit(solution)/shard_map/all_to_all | solution.py:46
  669.4 21.7 %collective-permute-done.5 = f32[2,256,256]{2,1,0:T(8,128)S(1)} collective-permute-done((f32[2,256,256]{2,1,0:T(8,128)S(1)}, f32[2,256,256]{2,1,0:T(8,128)S(1)}, u32[]{:S(2)}, u32[]{:S(2)}) %collective-permute-start.5) | collective-permute-done | bytes 524320 | tf_op jit(solution)/shard_map/ppermute | solution.py:21
  691.7 37.5 %all-gather.21.cloned.1.call-done = f32[8192,256]{1,0:T(8,128)} async-done(((f32[256,256]{1,0:T(8,128)}), f32[8192,256]{1,0:T(8,128)}) %all-gather.21.cloned.1.call-update) | async-done | bytes 8388624 | tf_op jit(solution)/shard_map/all_gather | solution.py:26
  733.2 86.8 %all-gather.23.cloned.1.call-done = f32[8192,256]{1,0:T(8,128)} async-done(((f32[256,256]{1,0:T(8,128)}), f32[8192,256]{1,0:T(8,128)}) %all-gather.23.cloned.1.call-update) | async-done | bytes 8388624 | tf_op jit(solution)/shard_map/all_gather | solution.py:26
  (138 shorter events, 127.6 us)
Async XLA Ops:
  43.5 22.5 %all-to-all-start.3 = ((f32[2,16,16,256]{3,2,0,1:T(8,128)}), f32[2,16,16,256]{3,2,0,1:T(8,128)S(1)}, u32[]{:S(2)}, u32[]{:S(2)}) async-start(f32[2,16,16,256]{3,2,0,1:T(8,128)} %broadcast_in_dim.91), calls=%async_computation.3 | async-start | bytes 1048576 | tf_op jit(solution)/shard_map/all_to_all | solution.py:46
  66.0 52.2 %copy-start = (f32[1,256,256]{2,1,0:T(8,128)S(1)}, f32[1,256,256]{2,1,0:T(8,128)}, u32[]{:S(2)}) copy-start(f32[1,256,256]{2,1,0:T(8,128)} %param.7) | copy-start | bytes 786436
  66.0 27.1 %all-to-all-start.1 = ((f32[32,16,256]{2,1,0:T(8,128)}), f32[32,16,256]{2,1,0:T(8,128)S(1)}, u32[]{:S(2)}, u32[]{:S(2)}) async-start(f32[32,16,256]{2,1,0:T(8,128)} %bitcast.5), calls=%async_computation.1 | async-start | bytes 1048576 | tf_op jit(solution)/shard_map/all_to_all | solution.py:56
  93.1 20.6 %all-to-all-start.4 = ((f32[32,16,256]{2,1,0:T(8,128)}), f32[32,16,256]{2,1,0:T(8,128)S(1)}, u32[]{:S(2)}, u32[]{:S(2)}) async-start(f32[32,16,256]{2,1,0:T(8,128)} %bitcast.12), calls=%async_computation.4 | async-start | bytes 1048576 | tf_op jit(solution)/shard_map/all_to_all | solution.py:56
  113.6 23.6 %all-to-all-start.2 = ((f32[2,16,16,256]{3,2,0,1:T(8,128)}), f32[2,16,16,256]{3,2,0,1:T(8,128)S(1)}, u32[]{:S(2)}, u32[]{:S(2)}) async-start(f32[2,16,16,256]{3,2,0,1:T(8,128)} %copy.27), calls=%async_computation.2 | async-start | bytes 1048576 | tf_op jit(solution)/shard_map/all_to_all | solution.py:46
  119.8 26.0 %copy-start.4 = (f32[1,2,1,256,256]{4,3,2,1,0:T(8,128)S(1)}, f32[1,2,1,256,256]{4,3,2,1,0:T(8,128)}, u32[]{:S(2)}) copy-start(f32[1,2,1,256,256]{4,3,2,1,0:T(8,128)} %param.5) | copy-start | bytes 1572868
  137.3 22.5 %all-to-all-start.5 = ((f32[2,16,16,256]{3,2,0,1:T(8,128)}), f32[2,16,16,256]{3,2,0,1:T(8,128)S(1)}, u32[]{:S(2)}, u32[]{:S(2)}) async-start(f32[2,16,16,256]{3,2,0,1:T(8,128)} %copy.31), calls=%async_computation.5 | async-start | bytes 1048576 | tf_op jit(solution)/shard_map/all_to_all | solution.py:46
  142.5 126.5 %all-gather.13.cloned.1.call-start = ((), (), s32[]{:S(2)}) async-start(), calls=%async_computation.12 | async-start | bytes 8650752 | tf_op jit(solution)/shard_map/all_gather | solution.py:26
  164.6 3.3 copy-start.1
  166.7 3.3 copy-start.8
  169.2 161.6 %all-gather.15.cloned.1.call-start = ((), (), s32[]{:S(2)}) async-start(), calls=%async_computation.13 | async-start | bytes 8650752 | tf_op jit(solution)/shard_map/all_gather | solution.py:26
  170.0 12.6 %collective-permute-start = (f32[2,256,256]{2,1,0:T(8,128)S(1)}, f32[2,256,256]{2,1,0:T(8,128)S(1)}, u32[]{:S(2)}, u32[]{:S(2)}) collective-permute-start(f32[2,256,256]{2,1,0:T(8,128)S(1)} %bitcast.248), channel_id=1, source_target_pairs={{0,1},{1,0},{2,3},{3,2},{4,5},{5,4},{6,7},{7,6},{8,9},{9,8},{10,11... | collective-permute-start | bytes 1572872 | tf_op jit(solution)/shard_map/ppermute | solution.py:15
  182.6 26.1 %collective-permute-start.1 = (f32[2,256,256]{2,1,0:T(8,128)S(1)}, f32[2,256,256]{2,1,0:T(8,128)S(1)}, u32[]{:S(2)}, u32[]{:S(2)}) collective-permute-start(f32[2,256,256]{2,1,0:T(8,128)S(1)} %collective-permute-done), channel_id=1, source_target_pairs={{0,2},{1,3},{2,0},{3,1},{4,6},{5,7},{6,4},{7,5},{8,10},{9,11},{10,... | collective-permute-start | bytes 1572872 | tf_op jit(solution)/shard_map/ppermute | solution.py:15
  208.7 32.3 %collective-permute-start.2 = (f32[2,256,256]{2,1,0:T(8,128)S(1)}, f32[2,256,256]{2,1,0:T(8,128)S(1)}, u32[]{:S(2)}, u32[]{:S(2)}) collective-permute-start(f32[2,256,256]{2,1,0:T(8,128)S(1)} %collective-permute-done.1), channel_id=1, source_target_pairs={{0,4},{1,5},{2,6},{3,7},{4,0},{5,1},{6,2},{7,3},{8,12},{9,13},{10,... | collective-permute-start | bytes 1572872 | tf_op jit(solution)/shard_map/ppermute | solution.py:15
  241.0 27.4 %collective-permute-start.3 = (f32[2,256,256]{2,1,0:T(8,128)S(1)}, f32[2,256,256]{2,1,0:T(8,128)S(1)}, u32[]{:S(2)}, u32[]{:S(2)}) collective-permute-start(f32[2,256,256]{2,1,0:T(8,128)S(1)} %collective-permute-done.2), channel_id=1, source_target_pairs={{0,8},{1,9},{2,10},{3,11},{4,12},{5,13},{6,14},{7,15},{8,0},{9,1},... | collective-permute-start | bytes 1572872 | tf_op jit(solution)/shard_map/ppermute | solution.py:15
  268.4 5.3 copy-start.5
  389.8 23.6 %all-to-all-start.8 = ((f32[2,16,16,256]{3,2,0,1:T(8,128)}), f32[2,16,16,256]{3,2,0,1:T(8,128)S(1)}, u32[]{:S(2)}, u32[]{:S(2)}) async-start(f32[2,16,16,256]{3,2,0,1:T(8,128)} %copy.36), calls=%async_computation.8 | async-start | bytes 1048576 | tf_op jit(solution)/shard_map/all_to_all | solution.py:46
  394.3 91.4 %all-gather.17.cloned.1.call-start = ((), (), s32[]{:S(2)}) async-start(), calls=%async_computation.14 | async-start | bytes 8650752 | tf_op jit(solution)/shard_map/all_gather | solution.py:26
  420.0 154.5 %all-gather.19.cloned.1.call-start = ((), (), s32[]{:S(2)}) async-start(), calls=%async_computation.15 | async-start | bytes 8650752 | tf_op jit(solution)/shard_map/all_gather | solution.py:26
  420.5 20.3 %collective-permute-start.4 = (f32[2,256,256]{2,1,0:T(8,128)S(1)}, f32[2,256,256]{2,1,0:T(8,128)}, u32[]{:S(2)}, u32[]{:S(2)}) collective-permute-start(f32[2,256,256]{2,1,0:T(8,128)S(1)} %copy-done.6), channel_id=1, source_target_pairs={{1,0},{2,1},{3,2},{4,3},{5,4},{6,5},{7,6},{8,7},{9,8},{10,9},{11,1... | collective-permute-start | bytes 1572872 | tf_op jit(solution)/shard_map/ppermute | solution.py:21
  633.4 23.6 %all-to-all-start.11 = ((f32[2,16,16,256]{3,2,0,1:T(8,128)}), f32[2,16,16,256]{3,2,0,1:T(8,128)S(1)}, u32[]{:S(2)}, u32[]{:S(2)}) async-start(f32[2,16,16,256]{3,2,0,1:T(8,128)} %copy.41), calls=%async_computation.11 | async-start | bytes 1048576 | tf_op jit(solution)/shard_map/all_to_all | solution.py:46
  638.0 91.3 %all-gather.21.cloned.1.call-start = ((), (), s32[]{:S(2)}) async-start(), calls=%async_computation.16 | async-start | bytes 8650752 | tf_op jit(solution)/shard_map/all_gather | solution.py:26
  663.5 156.4 %all-gather.23.cloned.1.call-start = ((), (), s32[]{:S(2)}) async-start(), calls=%async_computation.17 | async-start | bytes 8650752 | tf_op jit(solution)/shard_map/all_gather | solution.py:26
  664.1 27.0 %collective-permute-start.5 = (f32[2,256,256]{2,1,0:T(8,128)S(1)}, f32[2,256,256]{2,1,0:T(8,128)S(1)}, u32[]{:S(2)}, u32[]{:S(2)}) collective-permute-start(f32[2,256,256]{2,1,0:T(8,128)S(1)} %copy-done.7), channel_id=1, source_target_pairs={{2,0},{3,1},{4,2},{5,3},{6,4},{7,5},{8,6},{9,7},{10,8},{11,9},{12,... | collective-permute-start | bytes 1572872 | tf_op jit(solution)/shard_map/ppermute | solution.py:21
  (4 other events, 9.6 us)
Sparse Core Ops, SparseCore 0:
  169.3 67.7 all-gather.12
  239.3 91.3 all-gather.14
  420.1 65.5 all-gather.16
  487.7 86.7 all-gather.18
  663.6 65.5 all-gather.20
  731.2 88.6 all-gather.22
